TPU v7x, 256 devices: a whole 4x4x8 slice. The times are simulated.
256 devices in a mesh: row: 16 (over x, z_lo, core), col: 16 (over y, z_hi).
Axes of the slice: x: 4, y: 4, z: 8 (z_hi: 4, z_lo: 2; z = z_hi * 2 + z_lo), core: 2. Of those that a mesh axis runs over, the one named last changes fastest.
Arguments:
- ancestor_inverse: bfloat16 [32768, 32768], P('row', 'col'), may hold values from -0.03125 to 0.03125
- panel: bfloat16 [32768, 512], P(('row', 'col')), may hold values from -0.75 to 0.75
- structure: int32 [2, 128], replicated, may hold values 0 or 1
- diag_inverse: float32 [2, 256, 256], replicated, may hold values from -6 to 6
Outputs:
- upper: bfloat16 [32768, 512], P(('row', 'col'))
- diagonal: float32 [2, 256, 256], replicated
All inputs are finite; a program needn't handle non-finite values.
Results may differ from a plain program's by a relative error of at most 0.0014.
Values may be sent and summed in bfloat16 or wider, within the bound.
A program may use at most 64 MiB of HBM per device.

v0:
```python
import jax
import jax.numpy as jnp
from jax import lax
from jax.sharding import PartitionSpec as P


def row_keep(begin_row, length, structure, blk_width):
    blocks_all = structure.shape[1]
    indices = begin_row + jnp.arange(length, dtype=jnp.int32)
    owners = indices // blk_width
    onehot = (owners[:, None] == jnp.arange(blocks_all, dtype=jnp.int32)[None, :]).astype(
        jnp.float32
    )
    keeps = jnp.dot(onehot, structure.T.astype(jnp.float32), preferred_element_type=jnp.float32)
    return jnp.repeat(keeps, blk_width, axis=1)


def diag_part(lower, upper_rows, blk_width):
    snodes = upper_rows.shape[1] // blk_width
    lower_f = lower.astype(jnp.float32).reshape(lower.shape[0], snodes, blk_width)
    upper_f = upper_rows.reshape(upper_rows.shape[0], snodes, blk_width)
    return jnp.einsum("mkw,mkv->kwv", lower_f, upper_f, precision=lax.Precision.HIGHEST)


def local(ancestor_inverse, panel, structure, diag_inverse):
    blk_width = diag_inverse.shape[1]
    row_count = lax.axis_size("row")
    col_count = lax.axis_size("col")
    row_index = lax.axis_index("row")
    col_index = lax.axis_index("col")
    piece_rows = panel.shape[0]
    begin_own = (row_index * col_count + col_index) * piece_rows
    keep_own = row_keep(begin_own, piece_rows, structure, blk_width)
    masked = panel * keep_own.astype(jnp.bfloat16)
    flip = [
        (r * col_count + c, c * row_count + r) for r in range(row_count) for c in range(col_count)
    ]
    moved = lax.ppermute(masked, ("row", "col"), flip)
    col_block = lax.all_gather(moved, "row", axis=0, tiled=True)
    partial_rows = -jnp.dot(ancestor_inverse, col_block, preferred_element_type=jnp.float32)
    own_rows = lax.psum_scatter(partial_rows, "col", scatter_dimension=0, tiled=True)
    diag_sum = lax.psum(diag_part(masked, own_rows, blk_width), ("row", "col"))
    upper = (own_rows * keep_own).astype(jnp.bfloat16)
    diagonal = diag_inverse - diag_sum
    return (upper, diagonal)


def solution(mesh):
    return jax.shard_map(
        local,
        mesh=mesh,
        in_specs=(P("row", "col"), P(("row", "col"), None), P(), P()),
        out_specs=(P(("row", "col"), None), P()),
        check_vma=False,
    )
```

profile of v0, /device:TPU:2, one launch (start us, length us, event | category | flops | bytes accessed | tf_op | source)
XLA Modules:
  0.0 442.1 jit_solution(1587222471581334880)
XLA Ops:
  7.2 0.0 all-gather.2.cloned.1.call-start
  7.2 1.0 copy.6
  8.3 0.9 fusion.2
  9.2 3.5 collective-permute-start
  12.6 4.3 collective-permute-done
  17.0 0.0 copy-start.1
  17.0 0.7 copy-done.1
  17.6 0.0 all-gather.2.cloned.1.call-update
  17.6 0.0 reduce-scatter.2.cloned.1.call-start
  17.7 48.5 %all-gather.2.cloned.1.call-done = bf16[2048,512]{0,1:T(8,128)(2,1)} async-done(((bf16[128,512]{0,1:T(8,128)(2,1)}), bf16[2048,512]{0,1:T(8,128)(2,1)}) %all-gather.2.cloned.1.call-update) | async-done | bytes 2097168 | tf_op jit(solution)/shard_map/all_gather | solution.py:39
  66.2 10.5 %negate_bitcast_fusion = f32[2048,512]{0,1:T(8,128)} fusion(bf16[2048,512]{0,1:T(8,128)(2,1)} %all-gather.2.cloned.1.call-done, bf16[2048,2048]{1,0:T(8,128)(2,1)} %param.4), kind=kOutput, calls=%fused_computation | convolution fusion | flops 4296015872 | bytes 14680064 | tf_op jit(solution)/shard_map/dot_general | solution.py:40
  76.7 0.0 copy-start
  76.7 0.0 reduce-scatter.2.cloned.1.call-update
  76.7 0.0 all-reduce.2.cloned.1.call-start
  76.8 97.6 %reduce-scatter.2.cloned.1.call-done = f32[128,512]{0,1:T(8,128)} async-done(((f32[2048,512]{0,1:T(8,128)}), f32[128,512]{0,1:T(8,128)}) %reduce-scatter.2.cloned.1.call-update) | async-done | bytes 262160 | tf_op jit(solution)/shard_map/reduce_scatter | solution.py:41
  174.4 2.1 fusion.5
  176.5 0.0 all-reduce.2.cloned.1.call-update
  176.6 1.0 fusion
  177.5 0.8 copy.8
  178.3 255.4 %all-reduce.2.cloned.1.call-done = f32[2,256,256]{2,1,0:T(8,128)} async-done(((f32[2,256,256]{2,1,0:T(8,128)}), f32[2,256,256]{2,1,0:T(8,128)}) %all-reduce.2.cloned.1.call-update) | async-done | bytes 524304 | tf_op jit(solution)/shard_map/psum | solution.py:42
  433.7 0.0 copy-done
  433.7 1.9 sub.10
  (2 shorter events, 0.0 us)
Async XLA Ops:
  7.2 59.0 %all-gather.2.cloned.1.call-start = ((), (), s32[]{:S(2)}) async-start(), calls=%async_computation.1 | async-start | bytes 2228224 | tf_op jit(solution)/shard_map/all_gather | solution.py:39
  9.2 7.8 %collective-permute-start = (bf16[128,512]{0,1:T(8,128)(2,1)S(1)}, bf16[128,512]{0,1:T(8,128)(2,1)S(1)}, u32[]{:S(2)}, u32[]{:S(2)}) collective-permute-start(bf16[128,512]{0,1:T(8,128)(2,1)S(1)} %fusion.1), channel_id=1, source_target_pairs={{0,0},{1,16},{2,32},{3,48},{4,64},{5,80},{6,96},{7,112},{8,128},{9... | collective-permute-start | bytes 393224 | tf_op jit(solution)/shard_map/ppermute | solution.py:38
  17.0 0.7 copy-start.1
  17.6 156.8 %reduce-scatter.2.cloned.1.call-start = ((), (), s32[]{:S(2)}) async-start(), calls=%async_computation.2 | async-start | bytes 4456448 | tf_op jit(solution)/shard_map/reduce_scatter | solution.py:41
  76.7 357.0 %copy-start = (f32[2,256,256]{2,1,0:T(8,128)S(1)}, f32[2,256,256]{2,1,0:T(8,128)}, u32[]{:S(2)}) copy-start(f32[2,256,256]{2,1,0:T(8,128)} %param.7) | copy-start | bytes 1572868
  76.7 356.9 %all-reduce.2.cloned.1.call-start = ((), (), s32[]{:S(2)}) async-start(), calls=%async_computation.3 | async-start | bytes 1048576 | tf_op jit(solution)/shard_map/psum | solution.py:42
Sparse Core Ops, SparseCore 0:
  17.8 48.4 all-gather.1
  76.8 97.5 reduce-scatter.1
  180.4 253.1 all-reduce.1
where the time goes:
time: 442 us
  waiting for transfers between devices  406 us (92%)
  between operations  13.8 us (3%)
  matrix products  13.5 us (3%)
    psum x1, waiting for transfers between devices, local(): diag_sum = lax.psum(diag_part(masked, own_rows, blk_width), ('row', 'col'))  255 us
    reduce_scatter x1, waiting for transfers between devices, local(): lax.psum_scatter(partial_rows, 'col', scatter_dimension=0, tiled=True)  97.6 us
    all_gather x1, waiting for transfers between devices, local(): col_block = lax.all_gather(moved, 'row', axis=0, tiled=True)  48.5 us
    dot_general x1, matrix products, local(): jnp.dot(ancestor_inverse, col_block, preferred_element_type=jnp.float32)  10.5 us
  transfers between devices with their start and end apart: 4, of which 4 were waited for; matrix products, arithmetic and copies ran while one was open for 0% of the time, Pallas kernels for 0%

commit v1 on v0

--- a/solution.py
+++ b/solution.py
@@ -39,7 +39,7 @@
     col_block = lax.all_gather(moved, "row", axis=0, tiled=True)
     partial_rows = -jnp.dot(ancestor_inverse, col_block, preferred_element_type=jnp.float32)
     own_rows = lax.psum_scatter(partial_rows, "col", scatter_dimension=0, tiled=True)
-    diag_sum = lax.psum(diag_part(masked, own_rows, blk_width), ("row", "col"))
+    diag_sum = lax.psum(lax.psum(diag_part(masked, own_rows, blk_width), "col"), "row")
     upper = (own_rows * keep_own).astype(jnp.bfloat16)
     diagonal = diag_inverse - diag_sum
     return (upper, diagonal)

time: 442 us -> 476 us (1.077); the launches traced: 442 us -> 470 us
  waiting for transfers between devices: 406 us -> 434 us
    psum x1 -> x2, waiting for transfers between devices: 255 us -> 283 us  [the longest x1 167 us: local(): lax.psum(diag_part(masked, own_rows, blk_width), 'col')]
  transfers between devices with their start and end apart: 4 -> 5, of which waited for: 4 -> 5; matrix products, arithmetic and copies ran while one was open for 0% -> 0% of each run, Pallas kernels for 0% -> 0%
where the time goes in v1:
time: 476 us; the launch traced here: 470 us
  waiting for transfers between devices  434 us (91%)
  between operations  13.8 us (3%)
  matrix products  13.5 us (3%)
    psum x1, waiting for transfers between devices, local(): lax.psum(diag_part(masked, own_rows, blk_width), 'col')  167 us
    psum x1, waiting for transfers between devices, local(): lax.psum(lax.psum(diag_part(masked, own_rows, blk_width), 'col'), 'row')  116 us
    reduce_scatter x1, waiting for transfers between devices, local(): lax.psum_scatter(partial_rows, 'col', scatter_dimension=0, tiled=True)  97.6 us
    all_gather x1, waiting for transfers between devices, local(): col_block = lax.all_gather(moved, 'row', axis=0, tiled=True)  48.5 us
    dot_general x1, matrix products, local(): jnp.dot(ancestor_inverse, col_block, preferred_element_type=jnp.float32)  10.5 us
  transfers between devices with their start and end apart: 5, of which 5 were waited for; matrix products, arithmetic and copies ran while one was open for 0% of the time, Pallas kernels for 0%

profile of v1, /device:TPU:2, one launch (start us, length us, event | category | flops | bytes accessed | tf_op | source)
XLA Modules:
  0.0 470.0 jit_solution(18138829594782750900)
XLA Ops:
  7.2 0.0 all-gather.2.cloned.1.call-start
  7.2 1.0 copy.6
  8.3 0.9 fusion.2
  9.2 3.5 collective-permute-start
  12.6 4.3 collective-permute-done
  17.0 0.0 copy-start.1
  17.0 0.7 copy-done.1
  17.6 0.0 all-gather.2.cloned.1.call-update
  17.6 0.0 reduce-scatter.2.cloned.1.call-start
  17.7 48.5 %all-gather.2.cloned.1.call-done = bf16[2048,512]{0,1:T(8,128)(2,1)} async-done(((bf16[128,512]{0,1:T(8,128)(2,1)}), bf16[2048,512]{0,1:T(8,128)(2,1)}) %all-gather.2.cloned.1.call-update) | async-done | bytes 2097168 | tf_op jit(solution)/shard_map/all_gather | solution.py:39
  66.2 10.5 %negate_bitcast_fusion = f32[2048,512]{0,1:T(8,128)} fusion(bf16[2048,512]{0,1:T(8,128)(2,1)} %all-gather.2.cloned.1.call-done, bf16[2048,2048]{1,0:T(8,128)(2,1)} %param.4), kind=kOutput, calls=%fused_computation | convolution fusion | flops 4296015872 | bytes 14680064 | tf_op jit(solution)/shard_map/dot_general | solution.py:40
  76.7 0.0 copy-start
  76.7 0.0 reduce-scatter.2.cloned.1.call-update
  76.7 0.0 all-reduce.3.cloned.1.call-start
  76.8 97.6 %reduce-scatter.2.cloned.1.call-done = f32[128,512]{0,1:T(8,128)} async-done(((f32[2048,512]{0,1:T(8,128)}), f32[128,512]{0,1:T(8,128)}) %reduce-scatter.2.cloned.1.call-update) | async-done | bytes 262160 | tf_op jit(solution)/shard_map/reduce_scatter | solution.py:41
  174.4 2.1 fusion.5
  176.5 0.0 all-reduce.3.cloned.1.call-update
  176.6 0.0 all-reduce.5.cloned.1.call-start
  176.6 167.2 %all-reduce.3.cloned.1.call-done = f32[2,256,256]{2,1,0:T(8,128)} async-done(((f32[2,256,256]{2,1,0:T(8,128)}), f32[2,256,256]{2,1,0:T(8,128)}) %all-reduce.3.cloned.1.call-update) | async-done | bytes 524304 | tf_op jit(solution)/shard_map/psum | solution.py:42
  343.8 0.0 all-reduce.5.cloned.1.call-update
  343.9 1.0 fusion
  344.8 0.8 copy.8
  345.6 116.0 %all-reduce.5.cloned.1.call-done = f32[2,256,256]{2,1,0:T(8,128)} async-done(((f32[2,256,256]{2,1,0:T(8,128)}), f32[2,256,256]{2,1,0:T(8,128)}) %all-reduce.5.cloned.1.call-update) | async-done | bytes 524304 | tf_op jit(solution)/shard_map/psum | solution.py:42
  461.6 0.0 copy-done
  461.6 1.9 sub.10
  (2 shorter events, 0.0 us)
Async XLA Ops:
  7.2 59.0 %all-gather.2.cloned.1.call-start = ((), (), s32[]{:S(2)}) async-start(), calls=%async_computation.1 | async-start | bytes 2228224 | tf_op jit(solution)/shard_map/all_gather | solution.py:39
  9.2 7.8 %collective-permute-start = (bf16[128,512]{0,1:T(8,128)(2,1)S(1)}, bf16[128,512]{0,1:T(8,128)(2,1)S(1)}, u32[]{:S(2)}, u32[]{:S(2)}) collective-permute-start(bf16[128,512]{0,1:T(8,128)(2,1)S(1)} %fusion.1), channel_id=1, source_target_pairs={{0,0},{1,16},{2,32},{3,48},{4,64},{5,80},{6,96},{7,112},{8,128},{9... | collective-permute-start | bytes 393224 | tf_op jit(solution)/shard_map/ppermute | solution.py:38
  17.0 0.7 copy-start.1
  17.6 156.8 %reduce-scatter.2.cloned.1.call-start = ((), (), s32[]{:S(2)}) async-start(), calls=%async_computation.2 | async-start | bytes 4456448 | tf_op jit(solution)/shard_map/reduce_scatter | solution.py:41
  76.7 384.9 %copy-start = (f32[2,256,256]{2,1,0:T(8,128)S(1)}, f32[2,256,256]{2,1,0:T(8,128)}, u32[]{:S(2)}) copy-start(f32[2,256,256]{2,1,0:T(8,128)} %param.7) | copy-start | bytes 1572868
  76.7 267.1 %all-reduce.3.cloned.1.call-start = ((), (), s32[]{:S(2)}) async-start(), calls=%async_computation.3 | async-start | bytes 1048576 | tf_op jit(solution)/shard_map/psum | solution.py:42
  176.6 285.0 %all-reduce.5.cloned.1.call-start = ((), (), s32[]{:S(2)}) async-start(), calls=%async_computation.4 | async-start | bytes 1048576 | tf_op jit(solution)/shard_map/psum | solution.py:42
Sparse Core Ops, SparseCore 0:
  17.8 48.4 all-gather.1
  76.8 97.5 reduce-scatter.1
  177.6 166.1 all-reduce.2
  346.3 115.2 all-reduce.4

commit v2 on v0

--- a/solution.py
+++ b/solution.py
@@ -36,7 +36,9 @@
         (r * col_count + c, c * row_count + r) for r in range(row_count) for c in range(col_count)
     ]
     moved = lax.ppermute(masked, ("row", "col"), flip)
-    col_block = lax.all_gather(moved, "row", axis=0, tiled=True)
+    col_block = jnp.concatenate(
+        lax.all_to_all(jnp.stack([moved] * lax.axis_size("row")), "row", 0, 0), axis=0
+    )
     partial_rows = -jnp.dot(ancestor_inverse, col_block, preferred_element_type=jnp.float32)
     own_rows = lax.psum_scatter(partial_rows, "col", scatter_dimension=0, tiled=True)
     diag_sum = lax.psum(diag_part(masked, own_rows, blk_width), ("row", "col"))

time: 442 us -> 432 us (0.977)
  waiting for transfers between devices: 406 us -> 355 us
  blocking collectives: 0 us -> 41.5 us
    all_gather x1 -> x0, waiting for transfers between devices: 48.5 us -> none  [local(): col_block = lax.all_gather(moved, 'row', axis=0, tiled=True)]
    all_to_all x0 -> x1, blocking collectives: none -> 41.5 us  [local(): lax.all_to_all(jnp.stack([moved] * lax.axis_size('row')), 'row', 0, 0)]
  transfers between devices with their start and end apart: 4 -> 3, of which waited for: 4 -> 3; matrix products, arithmetic and copies ran while one was open for 0% -> 0% of each run, Pallas kernels for 0% -> 0%
where the time goes in v2:
time: 432 us; the launch traced here: 431 us
  waiting for transfers between devices  355 us (82%)
  blocking collectives  41.5 us (10%)
  between operations  14.1 us (3%)
  matrix products  12.6 us (3%)
    psum x1, waiting for transfers between devices, local(): diag_sum = lax.psum(diag_part(masked, own_rows, blk_width), ('row', 'col'))  255 us
    reduce_scatter x1, waiting for transfers between devices, local(): lax.psum_scatter(partial_rows, 'col', scatter_dimension=0, tiled=True)  94.9 us
    all_to_all x1, blocking collectives, local(): lax.all_to_all(jnp.stack([moved] * lax.axis_size('row')), 'row', 0, 0)  41.5 us
    dot_general x1, matrix products, local(): jnp.dot(ancestor_inverse, col_block, preferred_element_type=jnp.float32)  9.61 us
  transfers between devices with their start and end apart: 3, of which 3 were waited for; matrix products, arithmetic and copies ran while one was open for 0% of the time, Pallas kernels for 0%

profile of v2, /device:TPU:2, one launch (start us, length us, event | category | flops | bytes accessed | tf_op | source)
XLA Modules:
  0.0 431.3 jit_solution(409576046637895446)
XLA Ops:
  7.2 0.0 reduce-scatter.2.cloned.1.call-start
  7.2 1.0 copy.6
  8.3 0.9 fusion.2
  9.2 3.5 collective-permute-start
  12.6 4.3 collective-permute-done
  17.0 0.1 copy.7
  17.1 0.2 stack.2
  17.3 41.5 %all_to_all.5 = bf16[16,128,512]{2,1,0:T(8,128)(2,1)S(1)} all-to-all(bf16[16,128,512]{2,1,0:T(8,128)(2,1)S(1)} %stack.2), channel_id=1, replica_groups=mesh['row'=16,'col'=16] {'row'}, dimensions={0} | all-to-all | bytes 4194304 | tf_op jit(solution)/shard_map/all_to_all | solution.py:40
  58.8 9.6 %negate_bitcast_fusion = f32[2048,512]{0,1:T(8,128)} fusion(bf16[2048,512]{1,0:T(8,128)(2,1)S(1)} %bitcast.16, bf16[2048,2048]{1,0:T(8,128)(2,1)} %param.4), kind=kOutput, calls=%fused_computation | convolution fusion | flops 4296015872 | bytes 14680064 | tf_op jit(solution)/shard_map/dot_general | solution.py:42
  68.4 0.0 copy-start
  68.4 0.0 reduce-scatter.2.cloned.1.call-update
  68.4 0.0 all-reduce.2.cloned.1.call-start
  68.5 94.9 %reduce-scatter.2.cloned.1.call-done = f32[128,512]{0,1:T(8,128)} async-done(((f32[2048,512]{0,1:T(8,128)}), f32[128,512]{0,1:T(8,128)}) %reduce-scatter.2.cloned.1.call-update) | async-done | bytes 262160 | tf_op jit(solution)/shard_map/reduce_scatter | solution.py:43
  163.4 2.1 fusion.5
  165.5 0.0 all-reduce.2.cloned.1.call-update
  165.5 1.0 fusion
  166.5 0.8 copy.9
  167.3 255.3 %all-reduce.2.cloned.1.call-done = f32[2,256,256]{2,1,0:T(8,128)} async-done(((f32[2,256,256]{2,1,0:T(8,128)}), f32[2,256,256]{2,1,0:T(8,128)}) %all-reduce.2.cloned.1.call-update) | async-done | bytes 524304 | tf_op jit(solution)/shard_map/psum | solution.py:44
  422.6 0.0 copy-done
  422.6 1.9 sub.10
  (2 shorter events, 0.0 us)
Async XLA Ops:
  7.2 156.2 %reduce-scatter.2.cloned.1.call-start = ((), (), s32[]{:S(2)}) async-start(), calls=%async_computation.2 | async-start | bytes 4456448 | tf_op jit(solution)/shard_map/reduce_scatter | solution.py:43
  9.2 7.8 %collective-permute-start = (bf16[128,512]{0,1:T(8,128)(2,1)S(1)}, bf16[128,512]{0,1:T(8,128)(2,1)S(1)}, u32[]{:S(2)}, u32[]{:S(2)}) collective-permute-start(bf16[128,512]{0,1:T(8,128)(2,1)S(1)} %fusion.1), channel_id=1, source_target_pairs={{0,0},{1,16},{2,32},{3,48},{4,64},{5,80},{6,96},{7,112},{8,128},{9... | collective-permute-start | bytes 393224 | tf_op jit(solution)/shard_map/ppermute | solution.py:38
  68.4 354.2 %copy-start = (f32[2,256,256]{2,1,0:T(8,128)S(1)}, f32[2,256,256]{2,1,0:T(8,128)}, u32[]{:S(2)}) copy-start(f32[2,256,256]{2,1,0:T(8,128)} %param.7) | copy-start | bytes 1572868
  68.4 354.2 %all-reduce.2.cloned.1.call-start = ((), (), s32[]{:S(2)}) async-start(), calls=%async_computation.3 | async-start | bytes 1048576 | tf_op jit(solution)/shard_map/psum | solution.py:44
Sparse Core Ops, SparseCore 0:
  68.5 94.7 reduce-scatter.1
  169.4 253.1 all-reduce.1
